TPU v7x, 32 devices: a whole 2x2x4 slice. The times are simulated.
32 devices in a mesh: groups: 2 (over y), space: 4 (over z), disp: 4 (over x, core).
Axes of the slice: x: 2, y: 2, z: 4, core: 2. Of those that a mesh axis runs over, the one named last changes fastest.
Arguments:
- volume: bfloat16 [8, 16, 32, 256], P(None, 'disp', ('groups', 'space')), parts along dimension 2, may hold values from -6 to 6
- w_first: bfloat16 [3, 3, 3, 8, 8], replicated, may hold values from -0.4375 to 0.4375
- b_first: float32 [8], replicated, may hold values from -1 to 1
- w_second: bfloat16 [3, 3, 3, 8], replicated, may hold values from -0.4375 to 0.4375
- prior_logits: float32 [16, 32, 256], P('disp', ('groups', 'space')), parts along dimension 1, may hold values from -15 to 310
- cotangent: float32 [32, 256], P(('groups', 'space')), parts along dimension 0, may hold values from -24 to 24
Outputs:
- grad_volume: bfloat16 [8, 16, 32, 256], P(None, 'disp', ('groups', 'space')), parts along dimension 2
- grad_w_first: float32 [3, 3, 3, 16, 8], P(None, None, None, 'groups'), parts along dimension 3
- grad_b_first: float32 [16], P('groups'), parts along dimension 0
- grad_w_second: float32 [3, 3, 3, 16], P(None, None, None, 'groups'), parts along dimension 3
- disparity: float32 [32, 256], P(('groups', 'space')), parts along dimension 0
There are 2 independent parts, one for each index of `groups`. A program takes and returns all parts, laid end to end along the dimension named above; an argument that names none is the same for every part. Nothing has to cross between parts.
All inputs are finite; a program needn't handle non-finite values.
Results may differ from a plain program's by a relative error of at most 0.011.
Values may be sent and summed in bfloat16 or wider, within the bound.
No kernel may reach another device: no remote copies, remote signals or barrier semaphores. Data moves between devices by JAX's collectives and lax.ppermute only.
A program may use at most 64 MiB of HBM per device.

v0:
```python
import math
import jax
import jax.numpy as jnp
from jax import lax
from jax.sharding import PartitionSpec as P


def padded_2(cells, sides, width):
    for axis, dim in sides:
        count = lax.axis_size(axis)
        ends = count - 1
        head = lax.slice_in_dim(cells, 0, width, axis=dim)
        tail = lax.slice_in_dim(cells, cells.shape[dim] - width, cells.shape[dim], axis=dim)
        cells = jnp.concatenate(
            [
                lax.ppermute(tail, axis, [(i, (i + 1) % count) for i in range(ends)]),
                cells,
                lax.ppermute(head, axis, [((i + 1) % count, i) for i in range(ends)]),
            ],
            axis=dim,
        )
    return cells


def combined_all(value, axis, combine):
    everything = jax.tree.map(lambda part: lax.all_gather(part, axis), value)
    first = jax.tree.map(lambda part: part[0], everything)

    def step(k, so_far):
        return combine(so_far, jax.tree.map(lambda part: part[k], everything))

    return lax.fori_loop(1, lax.axis_size(axis), step, first)


def tap_stack(source, planes, rows, width):
    padded = jnp.pad(source, ((0, 0), (0, 0), (0, 0), (1, 1)))
    return jnp.concatenate(
        [
            padded[:, a : a + planes, b : b + rows, c : c + width]
            for a in range(3)
            for b in range(3)
            for c in range(3)
        ],
        axis=0,
    )


def correlate(source, kernel):
    planes = source.shape[1] - 2
    rows = source.shape[2] - 2
    width = source.shape[3]
    stacked = tap_stack(source, planes, rows, width)
    joined = jnp.concatenate(
        [kernel[a, b, c] for a in range(3) for b in range(3) for c in range(3)], axis=1
    )
    return jnp.einsum("oi,idhw->odhw", joined, stacked, preferred_element_type=jnp.float32)


def transposed(kernel):
    return jnp.swapaxes(kernel[::-1, ::-1, ::-1], 3, 4)


def kernel_grad(out_grad, source):
    planes = out_grad.shape[1]
    rows = out_grad.shape[2]
    width = out_grad.shape[3]
    stacked = tap_stack(source, planes, rows, width)
    product = jnp.einsum("odhw,kdhw->ok", out_grad, stacked, preferred_element_type=jnp.float32)
    outputs = product.shape[0]
    inputs = source.shape[0]
    return jnp.transpose(product.reshape(outputs, 3, 3, 3, inputs), (1, 2, 3, 0, 4))


def inside_mask(planes, rows, reach, plane_count, row_count):
    plane_index = (
        lax.axis_index("disp") * plane_count
        - reach
        + lax.broadcasted_iota(jnp.int32, (planes, rows, 1), 0)
    )
    row_index = (
        lax.axis_index("space") * row_count
        - reach
        + lax.broadcasted_iota(jnp.int32, (planes, rows, 1), 1)
    )
    keeper = (
        (plane_index >= 0)
        & (plane_index < plane_count * lax.axis_size("disp"))
        & (row_index >= 0)
        & (row_index < row_count * lax.axis_size("space"))
    )
    return keeper.astype(jnp.float32)


def combine_stats(first_part, second_part):
    highest = jnp.maximum(first_part[0], second_part[0])
    factor_one = jnp.exp(first_part[0] - highest)
    factor_two = jnp.exp(second_part[0] - highest)
    return (
        highest,
        first_part[1] * factor_one + second_part[1] * factor_two,
        first_part[2] * factor_one + second_part[2] * factor_two,
    )


def silu_grad(hidden_grad, pre_act):
    gate_sigmoid = jax.nn.sigmoid(pre_act)
    return (hidden_grad * gate_sigmoid * (1.0 + pre_act * (1.0 - gate_sigmoid))).astype(
        jnp.bfloat16
    )


def shards(volume, w_first, b_first, w_second, prior_logits, cotangent):
    plane_count = volume.shape[1]
    row_count = volume.shape[2]
    width = volume.shape[3]
    disp_size = lax.axis_size("disp")
    space_size = lax.axis_size("space")
    extended = padded_2(volume, (("space", 2), ("disp", 1)), 2)
    pre_act = correlate(extended, w_first) + b_first[:, None, None, None]
    inside = inside_mask(plane_count + 2, row_count + 2, 1, plane_count, row_count)
    hidden = (jax.nn.silu(pre_act) * inside[None]).astype(jnp.bfloat16)
    second_kernel = w_second[:, :, :, None, :]
    logits = correlate(hidden, second_kernel)[0] + prior_logits
    plane_total = plane_count * disp_size
    position = (
        lax.axis_index("disp") * plane_count
        + lax.broadcasted_iota(jnp.int32, (plane_count, 1, 1), 0)
    ).astype(jnp.float32)
    position = (position + 0.5) / plane_total
    local_top = jnp.max(logits, axis=0)
    local_exp = jnp.exp(logits - local_top[None])
    highest, summed, moment = combined_all(
        (local_top, jnp.sum(local_exp, axis=0), jnp.sum(local_exp * position, axis=0)),
        "disp",
        combine_stats,
    )
    disparity = moment / summed
    probability = jnp.exp(logits - highest[None]) / summed[None]
    score_grad = (cotangent[None] * probability * (position - disparity[None])).astype(jnp.bfloat16)
    second_grad = kernel_grad(score_grad[None], hidden)[:, :, :, 0, :]
    flipped_second = transposed(second_kernel)
    score_border = padded_2(score_grad, (("space", 1), ("disp", 0)), 2)
    hidden_grad = correlate(score_border[None], flipped_second)
    grad_border = silu_grad(hidden_grad, pre_act) * inside[None].astype(jnp.bfloat16)
    pre_grad = grad_border[:, 1:-1, 1:-1]
    volume_grad = correlate(grad_border, transposed(w_first)).astype(jnp.bfloat16)
    first_grad = kernel_grad(pre_grad, extended[:, 1:-1, 1:-1])
    bias_grad = jnp.sum(pre_grad, axis=(1, 2, 3), dtype=jnp.float32)
    grad_scale = 16.0 / math.sqrt(plane_total * row_count * space_size * width)
    first_sum, bias_sum, second_sum = lax.psum(
        (first_grad * grad_scale, bias_grad * grad_scale, second_grad * grad_scale),
        ("space", "disp"),
    )
    return (volume_grad, first_sum, bias_sum, second_sum, disparity)


def solution(mesh):
    return jax.shard_map(
        shards,
        mesh=mesh,
        in_specs=(
            P(None, "disp", ("groups", "space"), None),
            P(),
            P(),
            P(),
            P("disp", ("groups", "space"), None),
            P(("groups", "space"), None),
        ),
        out_specs=(
            P(None, "disp", ("groups", "space"), None),
            P(None, None, None, "groups", None),
            P("groups"),
            P(None, None, None, "groups"),
            P(("groups", "space"), None),
        ),
        check_vma=False,
    )
```

profile of v0, /device:TPU:0, one launch (start us, length us, event | category | flops | bytes accessed | tf_op | source)
XLA Modules:
  0.0 138.1 jit_solution(7539240962752502792)
XLA Ops:
  0.6 0.9 copy.121
  1.5 4.9 %collective-permute-start = (bf16[8,4,2,256]{3,0,2,1:T(8,128)(2,1)S(1)}, bf16[8,4,2,256]{3,0,2,1:T(8,128)(2,1)S(1)}, u32[]{:S(2)}, u32[]{:S(2)}) collective-permute-start(bf16[8,4,2,256]{3,0,2,1:T(8,128)(2,1)S(1)} %get-tuple-element.256), channel_id=1, source_target_pairs={{0,4},{4,8},{8,12},{1,5},{5,9},{9,13},{2,6},{6,10},{10,14},{3,7},{... | collective-permute-start | bytes 98312 | tf_op jit(solution)/shard_map/ppermute | solution.py:16
  6.5 1.3 collective-permute-start.1
  7.8 0.9 slice_bitcast_fusion.30
  8.6 0.8 slice_bitcast_fusion.31
  9.4 0.9 slice_bitcast_fusion.57
  10.3 0.8 slice_bitcast_fusion.76
  11.1 0.7 reverse.3
  11.9 0.9 copy.93
  15.7 0.1 concatenate.64
  15.8 0.1 concatenate.63
  15.9 0.1 concatenate.62
  16.1 0.9 constant_dynamic-update-slice_fusion.1
  17.0 1.5 %collective-permute-start.2 = (bf16[8,2,8,256]{3,0,2,1:T(8,128)(2,1)S(1)}, bf16[8,2,8,256]{3,0,2,1:T(8,128)(2,1)S(1)}, u32[]{:S(2)}, u32[]{:S(2)}) collective-permute-start(bf16[8,2,8,256]{3,0,2,1:T(8,128)(2,1)S(1)} %get-tuple-element.226), channel_id=1, source_target_pairs={{0,1},{1,2},{2,3},{4,5},{5,6},{6,7},{8,9},{9,10},{10,11},{12,13},{... | collective-permute-start | bytes 196616 | tf_op jit(solution)/shard_map/ppermute | solution.py:16
  18.5 1.3 collective-permute-start.3
  19.8 3.4 %collective-permute-done.3 = bf16[8,2,8,256]{3,0,2,1:T(8,128)(2,1)S(1)} collective-permute-done((bf16[8,2,8,256]{3,0,2,1:T(8,128)(2,1)S(1)}, bf16[8,2,8,256]{3,0,2,1:T(8,128)(2,1)S(1)}, u32[]{:S(2)}, u32[]{:S(2)}) %collective-permute-start.3) | collective-permute-done | bytes 65568 | tf_op jit(solution)/shard_map/ppermute | solution.py:18
  23.3 0.1 constant_dynamic-update-slice_fusion.27
  23.4 0.1 constant_dynamic-update-slice_fusion.26
  23.6 0.1 constant_dynamic-update-slice_fusion.24
  23.7 0.1 constant_dynamic-update-slice_fusion.23
  23.8 0.1 constant_dynamic-update-slice_fusion.21
  23.9 0.1 constant_dynamic-update-slice_fusion.20
  25.5 0.7 multiply_convert_fusion
  28.0 0.4 fusion.24
  28.5 6.8 %all-gather.5 = f32[4,4,256]{2,1,0:T(4,128)S(1)} all-gather(f32[1,4,256]{2,1,0:T(4,128)S(1)} %bitcast.306), channel_id=4, replica_groups=mesh['groups'=2,'space'=4,'disp'=4] {'disp'}, dimensions={0}, use_global_device_ids=true | all-gather | bytes 20480 | tf_op jit(solution)/shard_map/all_gather | solution.py:26
  35.2 5.2 %all-gather.4 = f32[4,4,256]{2,1,0:T(4,128)S(1)} all-gather(f32[1,4,256]{2,1,0:T(4,128)S(1)} %bitcast.305), channel_id=3, replica_groups=mesh['groups'=2,'space'=4,'disp'=4] {'disp'}, dimensions={0}, use_global_device_ids=true | all-gather | bytes 20480 | tf_op jit(solution)/shard_map/all_gather | solution.py:26
  40.4 5.2 %all-gather.3 = f32[4,4,256]{2,1,0:T(4,128)S(1)} all-gather(f32[1,4,256]{2,1,0:T(4,128)S(1)} %bitcast.304), channel_id=2, replica_groups=mesh['groups'=2,'space'=4,'disp'=4] {'disp'}, dimensions={0}, use_global_device_ids=true | all-gather | bytes 20480 | tf_op jit(solution)/shard_map/all_gather | solution.py:26
  45.6 0.2 while.19
  46.0 3.9 %fusion.3 = f32[1,3,3,3,8,1,1]{4,0,6,5,3,2,1:T(1,128)S(1)} fusion(bf16[3,3,3,8,4,4,256]{6,3,2,1,0,5,4:T(8,128)(2,1)S(1)} %bitcast.298, bf16[4,4,256,1,1,1,1]{2,1,0,3,4,5,6:T(4,128)(2,1)S(1)} %fusion.42), kind=kOutput, calls=%fused_computation.8 | convolution fusion | flops 1769472 | bytes 1778528 | tf_op jit(solution)/shard_map/odhw,kdhw->ok/dot_general | solution.py:68
  51.6 4.5 %collective-permute-start.4 = (bf16[4,2,256]{2,1,0:T(2,128)(2,1)S(1)}, bf16[4,2,256]{2,1,0:T(2,128)(2,1)S(1)}, u32[]{:S(2)}, u32[]{:S(2)}) collective-permute-start(bf16[4,2,256]{2,1,0:T(2,128)(2,1)S(1)} %get-tuple-element.367), channel_id=1, source_target_pairs={{0,4},{4,8},{8,12},{1,5},{5,9},{9,13},{2,6},{6,10},{10,14},{3,7},{... | collective-permute-start | bytes 12296 | tf_op jit(solution)/shard_map/ppermute | solution.py:16
  56.2 1.3 collective-permute-start.5
  57.5 4.2 %collective-permute-done.5 = bf16[4,2,256]{2,1,0:T(2,128)(2,1)S(1)} collective-permute-done((bf16[4,2,256]{2,1,0:T(2,128)(2,1)S(1)}, bf16[4,2,256]{2,1,0:T(2,128)(2,1)S(1)}, u32[]{:S(2)}, u32[]{:S(2)}) %collective-permute-start.5) | collective-permute-done | bytes 4128 | tf_op jit(solution)/shard_map/ppermute | solution.py:18
  61.7 1.3 collective-permute-start.6
  63.0 1.3 collective-permute-start.7
  64.4 3.2 %collective-permute-done.7 = bf16[2,8,256]{2,1,0:T(8,128)(2,1)S(1)} collective-permute-done((bf16[2,8,256]{2,1,0:T(8,128)(2,1)S(1)}, bf16[2,8,256]{2,1,0:T(8,128)(2,1)S(1)}, u32[]{:S(2)}, u32[]{:S(2)}) %collective-permute-start.7) | collective-permute-done | bytes 8224 | tf_op jit(solution)/shard_map/ppermute | solution.py:18
  67.7 0.6 pad_slice_fusion.93
  68.3 0.6 pad_slice_fusion.92
  68.9 0.2 fusion.32
  69.2 1.7 %concatenate.74 = bf16[27,6,6,256]{3,0,2,1:T(8,128)(2,1)S(1)} concatenate(bf16[1,6,6,256]{3,0,2,1:T(2,128)(2,1)S(1)} %get-tuple-element.254, bf16[1,6,6,256]{3,0,2,1:T(2,128)(2,1)S(1)} %get-tuple-element.253, bf16[1,6,6,256]{3,0,2,1:T(2,128)(2,1)S(1)} %get-tuple-element.229, bf16[1,6,6,256]{3,0,2,1:T(2,128)(2,1)S(1)} %get-tuple-element.230, ...), dimensions={0} | concatenate | bytes 995328 | tf_op jit(solution)/shard_map/concatenate | solution.py:37
  70.9 0.2 fusion.7
  71.1 0.1 convert_reduce_fusion
  71.4 1.0 copy-done.1
  72.4 0.6 fusion.8
  72.9 0.1 mul.133
  73.1 61.6 %all-reduce.5 = (f32[3,3,3,8,8]{4,2,1,0,3:T(4,128)S(1)}, f32[8]{0:T(128)}, f32[3,3,3,8]{3,2,1,0:T(4,128)}) all-reduce(f32[3,3,3,8,8]{4,2,1,0,3:T(4,128)S(1)} %bitcast.299, f32[8]{0:T(128)S(1)} %broadcast_multiply_fusion, f32[3,3,3,8]{3,2,1,0:T(4,128)S(1)} %bitcast_multiply_fusion.2), channel_id=1, replica_groups=mesh['groups'=2,'space'=4,'disp'=4] {'space','disp'}, use_global_device_ids=true, to_apply=%region_5.6 | all-reduce | flops 1952 | bytes 15616 | tf_op jit(solution)/shard_map/psum | solution.py:150
  134.7 0.7 copy.138
  137.1 0.4 convolution_convert_fusion
  137.4 0.7 copy.137
  (186 shorter events, 9.7 us)
Async XLA Ops:
  1.5 14.5 %collective-permute-start = (bf16[8,4,2,256]{3,0,2,1:T(8,128)(2,1)S(1)}, bf16[8,4,2,256]{3,0,2,1:T(8,128)(2,1)S(1)}, u32[]{:S(2)}, u32[]{:S(2)}) collective-permute-start(bf16[8,4,2,256]{3,0,2,1:T(8,128)(2,1)S(1)} %get-tuple-element.256), channel_id=1, source_target_pairs={{0,4},{4,8},{8,12},{1,5},{5,9},{9,13},{2,6},{6,10},{10,14},{3,7},{... | collective-permute-start | bytes 98312 | tf_op jit(solution)/shard_map/ppermute | solution.py:16
  6.5 10.5 %collective-permute-start.1 = (bf16[8,4,2,256]{3,0,2,1:T(8,128)(2,1)S(1)}, bf16[8,4,2,256]{3,0,2,1:T(8,128)(2,1)S(1)}, u32[]{:S(2)}, u32[]{:S(2)}) collective-permute-start(bf16[8,4,2,256]{3,0,2,1:T(8,128)(2,1)S(1)} %get-tuple-element.255), channel_id=1, source_target_pairs={{4,0},{8,4},{12,8},{5,1},{9,5},{13,9},{6,2},{10,6},{14,10},{7,3},{... | collective-permute-start | bytes 98312 | tf_op jit(solution)/shard_map/ppermute | solution.py:18
  17.0 2.8 %collective-permute-start.2 = (bf16[8,2,8,256]{3,0,2,1:T(8,128)(2,1)S(1)}, bf16[8,2,8,256]{3,0,2,1:T(8,128)(2,1)S(1)}, u32[]{:S(2)}, u32[]{:S(2)}) collective-permute-start(bf16[8,2,8,256]{3,0,2,1:T(8,128)(2,1)S(1)} %get-tuple-element.226), channel_id=1, source_target_pairs={{0,1},{1,2},{2,3},{4,5},{5,6},{6,7},{8,9},{9,10},{10,11},{12,13},{... | collective-permute-start | bytes 196616 | tf_op jit(solution)/shard_map/ppermute | solution.py:16
  18.5 4.7 %collective-permute-start.3 = (bf16[8,2,8,256]{3,0,2,1:T(8,128)(2,1)S(1)}, bf16[8,2,8,256]{3,0,2,1:T(8,128)(2,1)S(1)}, u32[]{:S(2)}, u32[]{:S(2)}) collective-permute-start(bf16[8,2,8,256]{3,0,2,1:T(8,128)(2,1)S(1)} %get-tuple-element.227), channel_id=1, source_target_pairs={{1,0},{2,1},{3,2},{5,4},{6,5},{7,6},{9,8},{10,9},{11,10},{13,12},{... | collective-permute-start | bytes 196616 | tf_op jit(solution)/shard_map/ppermute | solution.py:18
  24.7 0.8 copy-start.6
  27.4 1.0 copy-start.4
  27.6 18.2 %copy-start.5 = (f32[4,256]{1,0:T(4,128)S(1)}, f32[4,256]{1,0:T(4,128)}, u32[]{:S(2)}) copy-start(f32[4,256]{1,0:T(4,128)} %param.13) | copy-start | bytes 12292
  45.8 4.4 %copy-start.3 = (f32[4,256]{1,0:T(4,128)}, f32[4,256]{1,0:T(4,128)S(1)}, u32[]{:S(2)}) copy-start(f32[4,256]{1,0:T(4,128)S(1)} %div.23) | copy-start | bytes 12292
  49.9 0.9 copy-start.2
  51.6 5.9 %collective-permute-start.4 = (bf16[4,2,256]{2,1,0:T(2,128)(2,1)S(1)}, bf16[4,2,256]{2,1,0:T(2,128)(2,1)S(1)}, u32[]{:S(2)}, u32[]{:S(2)}) collective-permute-start(bf16[4,2,256]{2,1,0:T(2,128)(2,1)S(1)} %get-tuple-element.367), channel_id=1, source_target_pairs={{0,4},{4,8},{8,12},{1,5},{5,9},{9,13},{2,6},{6,10},{10,14},{3,7},{... | collective-permute-start | bytes 12296 | tf_op jit(solution)/shard_map/ppermute | solution.py:16
  56.2 5.5 %collective-permute-start.5 = (bf16[4,2,256]{2,1,0:T(2,128)(2,1)S(1)}, bf16[4,2,256]{2,1,0:T(2,128)(2,1)S(1)}, u32[]{:S(2)}, u32[]{:S(2)}) collective-permute-start(bf16[4,2,256]{2,1,0:T(2,128)(2,1)S(1)} %get-tuple-element.368), channel_id=1, source_target_pairs={{4,0},{8,4},{12,8},{5,1},{9,5},{13,9},{6,2},{10,6},{14,10},{7,3},{... | collective-permute-start | bytes 12296 | tf_op jit(solution)/shard_map/ppermute | solution.py:18
  61.7 2.7 %collective-permute-start.6 = (bf16[2,8,256]{2,1,0:T(8,128)(2,1)S(1)}, bf16[2,8,256]{2,1,0:T(8,128)(2,1)S(1)}, u32[]{:S(2)}, u32[]{:S(2)}) collective-permute-start(bf16[2,8,256]{2,1,0:T(8,128)(2,1)S(1)} %get-tuple-element.311), channel_id=1, source_target_pairs={{0,1},{1,2},{2,3},{4,5},{5,6},{6,7},{8,9},{9,10},{10,11},{12,13},{... | collective-permute-start | bytes 24584 | tf_op jit(solution)/shard_map/ppermute | solution.py:16
  63.0 4.6 %collective-permute-start.7 = (bf16[2,8,256]{2,1,0:T(8,128)(2,1)S(1)}, bf16[2,8,256]{2,1,0:T(8,128)(2,1)S(1)}, u32[]{:S(2)}, u32[]{:S(2)}) collective-permute-start(bf16[2,8,256]{2,1,0:T(8,128)(2,1)S(1)} %get-tuple-element.312), channel_id=1, source_target_pairs={{1,0},{2,1},{3,2},{5,4},{6,5},{7,6},{9,8},{10,9},{11,10},{13,12},{... | collective-permute-start | bytes 24584 | tf_op jit(solution)/shard_map/ppermute | solution.py:18
  64.4 3.2 %copy-start = (bf16[216,4,4,256]{3,0,2,1:T(8,128)(2,1)}, bf16[216,4,4,256]{3,0,2,1:T(8,128)(2,1)S(1)}, u32[]{:S(2)}) copy-start(bf16[216,4,4,256]{3,0,2,1:T(8,128)(2,1)S(1)} %constant_dynamic-update-slice_fusion.84) | copy-start | bytes 5308420
  70.9 1.5 %copy-start.1 = (bf16[216,4,4,256]{3,0,2,1:T(8,128)(2,1)S(1)}, bf16[216,4,4,256]{3,0,2,1:T(8,128)(2,1)}, u32[]{:S(2)}) copy-start(bf16[216,4,4,256]{3,0,2,1:T(8,128)(2,1)} %copy-done) | copy-start | bytes 5308420
where the time goes:
time: 139 us; the launch traced here: 138 us
  blocking collectives  78.7 us (57%)
  local copies, waits for them, and re-layouts  22.4 us (16%)
  starting transfers between devices  17.4 us (13%)
  waiting for transfers between devices  10.8 us (8%)
  matrix products  6.02 us (4%)
  between operations  1.86 us (1%)
    psum x1, blocking collectives, shards(): lax.psum((first_grad * grad_scale, bias_grad * grad_scale, second_grad *...  61.6 us
    all_gather x3, blocking collectives, combined_all(): everything = jax.tree.map(lambda part: lax.all_gather(part, axis), value)  17.1 us
    ppermute x4, starting transfers between devices, padded_2(): lax.ppermute(tail, axis, [(i, (i + 1) % count) for i in range(ends)])  12.2 us
    unnamed x109, local copies, waits for them, and re-layouts  11.4 us
    ppermute x4, waiting for transfers between devices, padded_2(): lax.ppermute(head, axis, [((i + 1) % count, i) for i in range(ends)])  10.8 us
    squeeze x35, local copies, waits for them, and re-layouts, correlate(): kernel[a, b, c]  5.99 us
    ppermute x4, starting transfers between devices, padded_2(): lax.ppermute(head, axis, [((i + 1) % count, i) for i in range(ends)])  5.17 us
    dot_general x2, matrix products, kernel_grad(): jnp.einsum('odhw,kdhw->ok', out_grad, stacked, preferred_element_type=jnp...  4.42 us
  transfers between devices with their start and end apart: 8, of which 3 were waited for; matrix products, arithmetic and copies ran while one was open for 7% of the time, Pallas kernels for 0%

commit v1 on v0

--- a/solution.py
+++ b/solution.py
@@ -3,6 +3,11 @@
 import jax.numpy as jnp
 from jax import lax
 from jax.sharding import PartitionSpec as P
+
+
+def by_each_axis(value_2, inner_axis, outer_axis):
+    half = lax.psum(value_2, inner_axis)
+    return lax.psum(half, outer_axis)
 
 
 def padded_2(cells, sides, width):
@@ -147,9 +152,8 @@
     first_grad = kernel_grad(pre_grad, extended[:, 1:-1, 1:-1])
     bias_grad = jnp.sum(pre_grad, axis=(1, 2, 3), dtype=jnp.float32)
     grad_scale = 16.0 / math.sqrt(plane_total * row_count * space_size * width)
-    first_sum, bias_sum, second_sum = lax.psum(
-        (first_grad * grad_scale, bias_grad * grad_scale, second_grad * grad_scale),
-        ("space", "disp"),
+    first_sum, bias_sum, second_sum = by_each_axis(
+        (first_grad * grad_scale, bias_grad * grad_scale, second_grad * grad_scale), "disp", "space"
     )
     return (volume_grad, first_sum, bias_sum, second_sum, disparity)
 

time: 139 us -> 112 us (0.81)
  blocking collectives: 78.7 us -> 52.3 us
    psum x1 -> x2, blocking collectives: 61.6 us -> 35.2 us  [the longest x1 20.9 us: by_each_axis(): return lax.psum(half, outer_axis)]
  transfers between devices with their start and end apart: 8 -> 8, of which waited for: 3 -> 3; matrix products, arithmetic and copies ran while one was open for 7% -> 8% of each run, Pallas kernels for 0% -> 0%
where the time goes in v1:
time: 112 us
  blocking collectives  52.3 us (47%)
  local copies, waits for them, and re-layouts  22.4 us (20%)
  starting transfers between devices  17.4 us (16%)
  waiting for transfers between devices  10.8 us (10%)
  matrix products  6.02 us (5%)
  between operations  1.86 us (2%)
    psum x1, blocking collectives, by_each_axis(): return lax.psum(half, outer_axis)  20.9 us
    all_gather x3, blocking collectives, combined_all(): everything = jax.tree.map(lambda part: lax.all_gather(part, axis), value)  17.1 us
    psum x1, blocking collectives, by_each_axis(): half = lax.psum(value_2, inner_axis)  14.4 us
    ppermute x4, starting transfers between devices, padded_2(): lax.ppermute(tail, axis, [(i, (i + 1) % count) for i in range(ends)])  12.2 us
    unnamed x109, local copies, waits for them, and re-layouts  11.4 us
    ppermute x4, waiting for transfers between devices, padded_2(): lax.ppermute(head, axis, [((i + 1) % count, i) for i in range(ends)])  10.8 us
    squeeze x35, local copies, waits for them, and re-layouts, correlate(): kernel[a, b, c]  5.99 us
    ppermute x4, starting transfers between devices, padded_2(): lax.ppermute(head, axis, [((i + 1) % count, i) for i in range(ends)])  5.17 us
  transfers between devices with their start and end apart: 8, of which 3 were waited for; matrix products, arithmetic and copies ran while one was open for 8% of the time, Pallas kernels for 0%

profile of v1, /device:TPU:0, one launch (start us, length us, event | category | flops | bytes accessed | tf_op | source)
XLA Modules:
  0.0 111.7 jit_solution(2006294606921522611)
XLA Ops:
  0.6 0.9 copy.121
  1.5 4.9 %collective-permute-start = (bf16[8,4,2,256]{3,0,2,1:T(8,128)(2,1)S(1)}, bf16[8,4,2,256]{3,0,2,1:T(8,128)(2,1)S(1)}, u32[]{:S(2)}, u32[]{:S(2)}) collective-permute-start(bf16[8,4,2,256]{3,0,2,1:T(8,128)(2,1)S(1)} %get-tuple-element.259), channel_id=1, source_target_pairs={{0,4},{4,8},{8,12},{1,5},{5,9},{9,13},{2,6},{6,10},{10,14},{3,7},{... | collective-permute-start | bytes 98312 | tf_op jit(solution)/shard_map/ppermute | solution.py:21
  6.5 1.3 %collective-permute-start.1 = (bf16[8,4,2,256]{3,0,2,1:T(8,128)(2,1)S(1)}, bf16[8,4,2,256]{3,0,2,1:T(8,128)(2,1)S(1)}, u32[]{:S(2)}, u32[]{:S(2)}) collective-permute-start(bf16[8,4,2,256]{3,0,2,1:T(8,128)(2,1)S(1)} %get-tuple-element.258), channel_id=1, source_target_pairs={{4,0},{8,4},{12,8},{5,1},{9,5},{13,9},{6,2},{10,6},{14,10},{7,3},{... | collective-permute-start | bytes 98312 | tf_op jit(solution)/shard_map/ppermute | solution.py:23
  7.8 0.9 slice_bitcast_fusion.30
  8.6 0.8 slice_bitcast_fusion.31
  9.4 0.9 slice_bitcast_fusion.57
  10.3 0.8 slice_bitcast_fusion.76
  11.1 0.7 reverse.3
  11.9 0.9 copy.93
  15.7 0.1 concatenate.64
  15.8 0.1 concatenate.63
  15.9 0.1 concatenate.62
  16.1 0.9 constant_dynamic-update-slice_fusion.1
  17.0 1.5 %collective-permute-start.2 = (bf16[8,2,8,256]{3,0,2,1:T(8,128)(2,1)S(1)}, bf16[8,2,8,256]{3,0,2,1:T(8,128)(2,1)S(1)}, u32[]{:S(2)}, u32[]{:S(2)}) collective-permute-start(bf16[8,2,8,256]{3,0,2,1:T(8,128)(2,1)S(1)} %get-tuple-element.229), channel_id=1, source_target_pairs={{0,1},{1,2},{2,3},{4,5},{5,6},{6,7},{8,9},{9,10},{10,11},{12,13},{... | collective-permute-start | bytes 196616 | tf_op jit(solution)/shard_map/ppermute | solution.py:21
  18.5 1.3 %collective-permute-start.3 = (bf16[8,2,8,256]{3,0,2,1:T(8,128)(2,1)S(1)}, bf16[8,2,8,256]{3,0,2,1:T(8,128)(2,1)S(1)}, u32[]{:S(2)}, u32[]{:S(2)}) collective-permute-start(bf16[8,2,8,256]{3,0,2,1:T(8,128)(2,1)S(1)} %get-tuple-element.230), channel_id=1, source_target_pairs={{1,0},{2,1},{3,2},{5,4},{6,5},{7,6},{9,8},{10,9},{11,10},{13,12},{... | collective-permute-start | bytes 196616 | tf_op jit(solution)/shard_map/ppermute | solution.py:23
  19.8 3.4 %collective-permute-done.3 = bf16[8,2,8,256]{3,0,2,1:T(8,128)(2,1)S(1)} collective-permute-done((bf16[8,2,8,256]{3,0,2,1:T(8,128)(2,1)S(1)}, bf16[8,2,8,256]{3,0,2,1:T(8,128)(2,1)S(1)}, u32[]{:S(2)}, u32[]{:S(2)}) %collective-permute-start.3) | collective-permute-done | bytes 65568 | tf_op jit(solution)/shard_map/ppermute | solution.py:23
  23.3 0.1 constant_dynamic-update-slice_fusion.27
  23.4 0.1 constant_dynamic-update-slice_fusion.26
  23.6 0.1 constant_dynamic-update-slice_fusion.24
  23.7 0.1 constant_dynamic-update-slice_fusion.23
  23.8 0.1 constant_dynamic-update-slice_fusion.21
  25.5 0.7 multiply_convert_fusion
  28.0 0.4 fusion.24
  28.5 6.8 %all-gather.5 = f32[4,4,256]{2,1,0:T(4,128)S(1)} all-gather(f32[1,4,256]{2,1,0:T(4,128)S(1)} %bitcast.306), channel_id=4, replica_groups=mesh['groups'=2,'space'=4,'disp'=4] {'disp'}, dimensions={0}, use_global_device_ids=true | all-gather | bytes 20480 | tf_op jit(solution)/shard_map/all_gather | solution.py:31
  35.2 5.2 %all-gather.4 = f32[4,4,256]{2,1,0:T(4,128)S(1)} all-gather(f32[1,4,256]{2,1,0:T(4,128)S(1)} %bitcast.305), channel_id=3, replica_groups=mesh['groups'=2,'space'=4,'disp'=4] {'disp'}, dimensions={0}, use_global_device_ids=true | all-gather | bytes 20480 | tf_op jit(solution)/shard_map/all_gather | solution.py:31
  40.4 5.2 %all-gather.3 = f32[4,4,256]{2,1,0:T(4,128)S(1)} all-gather(f32[1,4,256]{2,1,0:T(4,128)S(1)} %bitcast.304), channel_id=2, replica_groups=mesh['groups'=2,'space'=4,'disp'=4] {'disp'}, dimensions={0}, use_global_device_ids=true | all-gather | bytes 20480 | tf_op jit(solution)/shard_map/all_gather | solution.py:31
  45.6 0.2 while.19
  46.0 3.9 %fusion.3 = f32[1,3,3,3,8,1,1]{4,0,6,5,3,2,1:T(1,128)S(1)} fusion(bf16[3,3,3,8,4,4,256]{6,3,2,1,0,5,4:T(8,128)(2,1)S(1)} %bitcast.298, bf16[4,4,256,1,1,1,1]{2,1,0,3,4,5,6:T(4,128)(2,1)S(1)} %fusion.42), kind=kOutput, calls=%fused_computation.8 | convolution fusion | flops 1769472 | bytes 1778528 | tf_op jit(solution)/shard_map/odhw,kdhw->ok/dot_general | solution.py:73
  51.6 4.5 %collective-permute-start.4 = (bf16[4,2,256]{2,1,0:T(2,128)(2,1)S(1)}, bf16[4,2,256]{2,1,0:T(2,128)(2,1)S(1)}, u32[]{:S(2)}, u32[]{:S(2)}) collective-permute-start(bf16[4,2,256]{2,1,0:T(2,128)(2,1)S(1)} %get-tuple-element.370), channel_id=1, source_target_pairs={{0,4},{4,8},{8,12},{1,5},{5,9},{9,13},{2,6},{6,10},{10,14},{3,7},{... | collective-permute-start | bytes 12296 | tf_op jit(solution)/shard_map/ppermute | solution.py:21
  56.2 1.3 %collective-permute-start.5 = (bf16[4,2,256]{2,1,0:T(2,128)(2,1)S(1)}, bf16[4,2,256]{2,1,0:T(2,128)(2,1)S(1)}, u32[]{:S(2)}, u32[]{:S(2)}) collective-permute-start(bf16[4,2,256]{2,1,0:T(2,128)(2,1)S(1)} %get-tuple-element.371), channel_id=1, source_target_pairs={{4,0},{8,4},{12,8},{5,1},{9,5},{13,9},{6,2},{10,6},{14,10},{7,3},{... | collective-permute-start | bytes 12296 | tf_op jit(solution)/shard_map/ppermute | solution.py:23
  57.5 4.2 %collective-permute-done.5 = bf16[4,2,256]{2,1,0:T(2,128)(2,1)S(1)} collective-permute-done((bf16[4,2,256]{2,1,0:T(2,128)(2,1)S(1)}, bf16[4,2,256]{2,1,0:T(2,128)(2,1)S(1)}, u32[]{:S(2)}, u32[]{:S(2)}) %collective-permute-start.5) | collective-permute-done | bytes 4128 | tf_op jit(solution)/shard_map/ppermute | solution.py:23
  61.7 1.3 %collective-permute-start.6 = (bf16[2,8,256]{2,1,0:T(8,128)(2,1)S(1)}, bf16[2,8,256]{2,1,0:T(8,128)(2,1)S(1)}, u32[]{:S(2)}, u32[]{:S(2)}) collective-permute-start(bf16[2,8,256]{2,1,0:T(8,128)(2,1)S(1)} %get-tuple-element.314), channel_id=1, source_target_pairs={{0,1},{1,2},{2,3},{4,5},{5,6},{6,7},{8,9},{9,10},{10,11},{12,13},{... | collective-permute-start | bytes 24584 | tf_op jit(solution)/shard_map/ppermute | solution.py:21
  63.0 1.3 %collective-permute-start.7 = (bf16[2,8,256]{2,1,0:T(8,128)(2,1)S(1)}, bf16[2,8,256]{2,1,0:T(8,128)(2,1)S(1)}, u32[]{:S(2)}, u32[]{:S(2)}) collective-permute-start(bf16[2,8,256]{2,1,0:T(8,128)(2,1)S(1)} %get-tuple-element.315), channel_id=1, source_target_pairs={{1,0},{2,1},{3,2},{5,4},{6,5},{7,6},{9,8},{10,9},{11,10},{13,12},{... | collective-permute-start | bytes 24584 | tf_op jit(solution)/shard_map/ppermute | solution.py:23
  64.4 3.2 %collective-permute-done.7 = bf16[2,8,256]{2,1,0:T(8,128)(2,1)S(1)} collective-permute-done((bf16[2,8,256]{2,1,0:T(8,128)(2,1)S(1)}, bf16[2,8,256]{2,1,0:T(8,128)(2,1)S(1)}, u32[]{:S(2)}, u32[]{:S(2)}) %collective-permute-start.7) | collective-permute-done | bytes 8224 | tf_op jit(solution)/shard_map/ppermute | solution.py:23
  67.7 0.6 pad_slice_fusion.93
  68.3 0.6 pad_slice_fusion.92
  68.9 0.2 fusion.32
  69.2 1.7 %concatenate.74 = bf16[27,6,6,256]{3,0,2,1:T(8,128)(2,1)S(1)} concatenate(bf16[1,6,6,256]{3,0,2,1:T(2,128)(2,1)S(1)} %get-tuple-element.257, bf16[1,6,6,256]{3,0,2,1:T(2,128)(2,1)S(1)} %get-tuple-element.256, bf16[1,6,6,256]{3,0,2,1:T(2,128)(2,1)S(1)} %get-tuple-element.232, bf16[1,6,6,256]{3,0,2,1:T(2,128)(2,1)S(1)} %get-tuple-element.233, ...), dimensions={0} | concatenate | bytes 995328 | tf_op jit(solution)/shard_map/concatenate | solution.py:42
  70.9 0.2 fusion.7
  71.1 0.1 convert_reduce_fusion
  71.4 1.0 copy-done.1
  72.4 0.6 fusion.8
  72.9 0.1 mul.133
  73.1 14.4 %all-reduce.5 = (f32[3,3,3,8,8]{4,2,1,0,3:T(4,128)S(1)}, f32[8]{0:T(128)S(1)}, f32[3,3,3,8]{3,2,1,0:T(4,128)S(1)}) all-reduce(f32[3,3,3,8,8]{4,2,1,0,3:T(4,128)S(1)} %bitcast.299, f32[8]{0:T(128)S(1)} %broadcast_multiply_fusion, f32[3,3,3,8]{3,2,1,0:T(4,128)S(1)} %bitcast_multiply_fusion.2), channel_id=1, replica_groups=mesh['groups'=2,'space'=4,'disp'=4] {'disp'}, use_global_device_ids=true, to_apply=%region_5.6 | all-reduce | flops 1952 | bytes 15616 | tf_op jit(solution)/shard_map/psum | solution.py:9
  87.5 20.9 %all-reduce.6 = (f32[3,3,3,8,8]{4,2,1,0,3:T(4,128)S(1)}, f32[8]{0:T(128)}, f32[3,3,3,8]{3,2,1,0:T(4,128)}) all-reduce(f32[3,3,3,8,8]{4,2,1,0,3:T(4,128)S(1)} %get-tuple-element.217, f32[8]{0:T(128)S(1)} %get-tuple-element.218, f32[3,3,3,8]{3,2,1,0:T(4,128)S(1)} %get-tuple-element.219), channel_id=1, replica_groups=mesh['groups'=2,'space'=4,'disp'=4] {'space'}, use_global_device_ids=true, to_apply=%region_6.7 | all-reduce | flops 1952 | bytes 15616 | tf_op jit(solution)/shard_map/psum | solution.py:10
  108.3 0.7 copy.138
  110.7 0.4 convolution_convert_fusion
  111.1 0.7 copy.137
  (187 shorter events, 9.8 us)
Async XLA Ops:
  1.5 14.5 %collective-permute-start = (bf16[8,4,2,256]{3,0,2,1:T(8,128)(2,1)S(1)}, bf16[8,4,2,256]{3,0,2,1:T(8,128)(2,1)S(1)}, u32[]{:S(2)}, u32[]{:S(2)}) collective-permute-start(bf16[8,4,2,256]{3,0,2,1:T(8,128)(2,1)S(1)} %get-tuple-element.259), channel_id=1, source_target_pairs={{0,4},{4,8},{8,12},{1,5},{5,9},{9,13},{2,6},{6,10},{10,14},{3,7},{... | collective-permute-start | bytes 98312 | tf_op jit(solution)/shard_map/ppermute | solution.py:21
  6.5 10.5 %collective-permute-start.1 = (bf16[8,4,2,256]{3,0,2,1:T(8,128)(2,1)S(1)}, bf16[8,4,2,256]{3,0,2,1:T(8,128)(2,1)S(1)}, u32[]{:S(2)}, u32[]{:S(2)}) collective-permute-start(bf16[8,4,2,256]{3,0,2,1:T(8,128)(2,1)S(1)} %get-tuple-element.258), channel_id=1, source_target_pairs={{4,0},{8,4},{12,8},{5,1},{9,5},{13,9},{6,2},{10,6},{14,10},{7,3},{... | collective-permute-start | bytes 98312 | tf_op jit(solution)/shard_map/ppermute | solution.py:23
  17.0 2.8 %collective-permute-start.2 = (bf16[8,2,8,256]{3,0,2,1:T(8,128)(2,1)S(1)}, bf16[8,2,8,256]{3,0,2,1:T(8,128)(2,1)S(1)}, u32[]{:S(2)}, u32[]{:S(2)}) collective-permute-start(bf16[8,2,8,256]{3,0,2,1:T(8,128)(2,1)S(1)} %get-tuple-element.229), channel_id=1, source_target_pairs={{0,1},{1,2},{2,3},{4,5},{5,6},{6,7},{8,9},{9,10},{10,11},{12,13},{... | collective-permute-start | bytes 196616 | tf_op jit(solution)/shard_map/ppermute | solution.py:21
  18.5 4.7 %collective-permute-start.3 = (bf16[8,2,8,256]{3,0,2,1:T(8,128)(2,1)S(1)}, bf16[8,2,8,256]{3,0,2,1:T(8,128)(2,1)S(1)}, u32[]{:S(2)}, u32[]{:S(2)}) collective-permute-start(bf16[8,2,8,256]{3,0,2,1:T(8,128)(2,1)S(1)} %get-tuple-element.230), channel_id=1, source_target_pairs={{1,0},{2,1},{3,2},{5,4},{6,5},{7,6},{9,8},{10,9},{11,10},{13,12},{... | collective-permute-start | bytes 196616 | tf_op jit(solution)/shard_map/ppermute | solution.py:23
  24.7 0.8 copy-start.6
  27.4 1.0 copy-start.4
  27.6 18.2 %copy-start.5 = (f32[4,256]{1,0:T(4,128)S(1)}, f32[4,256]{1,0:T(4,128)}, u32[]{:S(2)}) copy-start(f32[4,256]{1,0:T(4,128)} %param.13) | copy-start | bytes 12292
  45.8 4.4 %copy-start.3 = (f32[4,256]{1,0:T(4,128)}, f32[4,256]{1,0:T(4,128)S(1)}, u32[]{:S(2)}) copy-start(f32[4,256]{1,0:T(4,128)S(1)} %div.23) | copy-start | bytes 12292
  49.9 0.9 copy-start.2
  51.6 5.9 %collective-permute-start.4 = (bf16[4,2,256]{2,1,0:T(2,128)(2,1)S(1)}, bf16[4,2,256]{2,1,0:T(2,128)(2,1)S(1)}, u32[]{:S(2)}, u32[]{:S(2)}) collective-permute-start(bf16[4,2,256]{2,1,0:T(2,128)(2,1)S(1)} %get-tuple-element.370), channel_id=1, source_target_pairs={{0,4},{4,8},{8,12},{1,5},{5,9},{9,13},{2,6},{6,10},{10,14},{3,7},{... | collective-permute-start | bytes 12296 | tf_op jit(solution)/shard_map/ppermute | solution.py:21
  56.2 5.5 %collective-permute-start.5 = (bf16[4,2,256]{2,1,0:T(2,128)(2,1)S(1)}, bf16[4,2,256]{2,1,0:T(2,128)(2,1)S(1)}, u32[]{:S(2)}, u32[]{:S(2)}) collective-permute-start(bf16[4,2,256]{2,1,0:T(2,128)(2,1)S(1)} %get-tuple-element.371), channel_id=1, source_target_pairs={{4,0},{8,4},{12,8},{5,1},{9,5},{13,9},{6,2},{10,6},{14,10},{7,3},{... | collective-permute-start | bytes 12296 | tf_op jit(solution)/shard_map/ppermute | solution.py:23
  61.7 2.7 %collective-permute-start.6 = (bf16[2,8,256]{2,1,0:T(8,128)(2,1)S(1)}, bf16[2,8,256]{2,1,0:T(8,128)(2,1)S(1)}, u32[]{:S(2)}, u32[]{:S(2)}) collective-permute-start(bf16[2,8,256]{2,1,0:T(8,128)(2,1)S(1)} %get-tuple-element.314), channel_id=1, source_target_pairs={{0,1},{1,2},{2,3},{4,5},{5,6},{6,7},{8,9},{9,10},{10,11},{12,13},{... | collective-permute-start | bytes 24584 | tf_op jit(solution)/shard_map/ppermute | solution.py:21
  63.0 4.6 %collective-permute-start.7 = (bf16[2,8,256]{2,1,0:T(8,128)(2,1)S(1)}, bf16[2,8,256]{2,1,0:T(8,128)(2,1)S(1)}, u32[]{:S(2)}, u32[]{:S(2)}) collective-permute-start(bf16[2,8,256]{2,1,0:T(8,128)(2,1)S(1)} %get-tuple-element.315), channel_id=1, source_target_pairs={{1,0},{2,1},{3,2},{5,4},{6,5},{7,6},{9,8},{10,9},{11,10},{13,12},{... | collective-permute-start | bytes 24584 | tf_op jit(solution)/shard_map/ppermute | solution.py:23
  64.4 3.2 %copy-start = (bf16[216,4,4,256]{3,0,2,1:T(8,128)(2,1)}, bf16[216,4,4,256]{3,0,2,1:T(8,128)(2,1)S(1)}, u32[]{:S(2)}) copy-start(bf16[216,4,4,256]{3,0,2,1:T(8,128)(2,1)S(1)} %constant_dynamic-update-slice_fusion.84) | copy-start | bytes 5308420
  70.9 1.5 %copy-start.1 = (bf16[216,4,4,256]{3,0,2,1:T(8,128)(2,1)S(1)}, bf16[216,4,4,256]{3,0,2,1:T(8,128)(2,1)}, u32[]{:S(2)}) copy-start(bf16[216,4,4,256]{3,0,2,1:T(8,128)(2,1)} %copy-done) | copy-start | bytes 5308420
